TPU v7x, 32 devices: a whole 2x2x4 slice. The times are simulated.
32 devices in a mesh: row: 8 (over y, x, core), col: 4 (over z).
Axes of the slice: x: 2, y: 2, z: 4, core: 2. Of those that a mesh axis runs over, the one named last changes fastest.
Arguments:
- earlier_blocks: bfloat16 [32, 8, 128, 128], P('row', 'col'), may hold values from -0.5 to 0.5
- later_blocks: bfloat16 [8, 32, 128, 128], P('row', 'col'), may hold values from -6 to 6
- earlier_pattern: int32 [32, 8], P('row', 'col'), may hold values from 0 to 1, as said below
- later_pattern: int32 [8, 32], P('row', 'col'), may hold values from 0 to 1, as said below
- triples: int32 [32, 32, 48], P('row', 'col'), may hold values from 0 to 7
Outputs:
- composed: float32 [32, 32, 128, 128], P('row', 'col')
Inputs may be any that keep to these rules, and one draw needn't show every extreme that they name: `earlier_pattern`: in each aligned share of 4 x 2 entries held by one device, at most 4 entries are 1, and exactly 4 in some share. `later_pattern`: in each aligned share of 1 x 8 entries held by one device, at most 4 entries are 1, and exactly 4 in some share.
All inputs are finite; a program needn't handle non-finite values.
Results may differ from a plain program's by a relative error of at most 0.0003.
Values may be sent and summed in bfloat16 or wider, within the bound.
A program may use at most 256 MiB of HBM per device.

v0:
```python
import jax
import jax.numpy as jnp
from jax import lax
from jax.sharding import PartitionSpec as P


def compose_blocks(earlier_full, later_full, triples):
    count_rows = triples.shape[0]
    middle = earlier_full.shape[1]
    middle_numbers = jnp.arange(middle, dtype=jnp.int32)
    counts = jnp.sum(
        (triples[:, :, :, None] == middle_numbers[None, None, None, :]).astype(jnp.float32), axis=2
    )
    results = []
    for row_number in range(count_rows):
        products = jnp.einsum(
            "kab,kjbc->kjac",
            earlier_full[row_number],
            later_full,
            preferred_element_type=jnp.float32,
        )
        results.append(
            jnp.einsum(
                "jk,kjac->jac", counts[row_number], products, precision=lax.Precision.HIGHEST
            )
        )
    return jnp.stack(results, axis=0)


def on_device(earlier_blocks, later_blocks, earlier_pattern, later_pattern, triples):
    masked_early = earlier_blocks * earlier_pattern[:, :, None, None].astype(earlier_blocks.dtype)
    earlier_full = lax.all_gather(masked_early, "col", axis=1, tiled=True)
    masked_late = later_blocks * later_pattern[:, :, None, None].astype(later_blocks.dtype)
    later_full = lax.all_gather(masked_late, "row", axis=0, tiled=True)
    return compose_blocks(earlier_full, later_full, triples)


def solution(mesh):
    return jax.shard_map(
        on_device,
        mesh=mesh,
        in_specs=(
            P("row", "col", None, None),
            P("row", "col", None, None),
            P("row", "col"),
            P("row", "col"),
            P("row", "col", None),
        ),
        out_specs=P("row", "col", None, None),
        check_vma=False,
    )
```

profile of v0, /device:TPU:0, one launch (start us, length us, event | category | flops | bytes accessed | tf_op | source)
XLA Modules:
  0.0 129.0 jit_solution(241129378847575528)
XLA Ops:
  6.5 0.7 convert_element_type.21
  7.2 0.1 copy.8
  7.3 1.7 %broadcast_multiply_fusion = bf16[4,2,128,128]{3,2,1,0:T(8,128)(2,1)} fusion(bf16[4,2,128,128]{3,2,1,0:T(8,128)(2,1)} %param.5, bf16[4,2]{1,0:T(4,128)(2,1)S(1)} %copy.8), kind=kLoop, calls=%fused_computation.9 | loop fusion | flops 131072 | bytes 524304 | tf_op jit(solution)/shard_map/mul | solution.py:31
  9.1 0.0 all-gather.5.cloned.1.call-update
  9.1 0.0 all-gather.3.cloned.1.call-start
  9.1 0.7 convert_bitcast_fusion
  9.8 1.7 %broadcast_multiply_fusion.1 = bf16[1,8,128,128]{3,2,1,0:T(8,128)(2,1)} fusion(bf16[1,8,128,128]{3,2,1,0:T(8,128)(2,1)} %param.6, bf16[8]{0:T(256)(128)(2,1)S(1)} %convert_bitcast_fusion), kind=kLoop, calls=%fused_computation.10 | loop fusion | flops 131072 | bytes 524304 | tf_op jit(solution)/shard_map/mul | solution.py:33
  11.5 0.0 all-gather.3.cloned.1.call-update
  11.6 0.8 convert_reduce_fusion
  12.4 27.5 %all-gather.5.cloned.1.call-done = bf16[4,8,128,128]{3,2,1,0:T(8,128)(2,1)} async-done(((bf16[4,2,128,128]{3,2,1,0:T(8,128)(2,1)}), bf16[4,8,128,128]{3,2,1,0:T(8,128)(2,1)}) %all-gather.5.cloned.1.call-update) | async-done | bytes 1048592 | tf_op jit(solution)/shard_map/all_gather | solution.py:32
  40.0 29.1 %all-gather.3.cloned.1.call-done = bf16[8,8,128,128]{3,2,1,0:T(8,128)(2,1)} async-done(((bf16[1,8,128,128]{3,2,1,0:T(8,128)(2,1)}), bf16[8,8,128,128]{3,2,1,0:T(8,128)(2,1)}) %all-gather.3.cloned.1.call-update) | async-done | bytes 2097168 | tf_op jit(solution)/shard_map/all_gather | solution.py:34
  69.0 4.4 %convolution_bitcast_fusion = f32[8,8,128,128]{2,3,1,0:T(8,128)} fusion(bf16[8,8,128,128]{3,2,1,0:T(8,128)(2,1)} %all-gather.3.cloned.1.call-done, bf16[4,8,128,128]{3,2,1,0:T(8,128)(2,1)} %all-gather.5.cloned.1.call-done), kind=kOutput, calls=%fused_computation | convolution fusion | flops 268435456 | bytes 6553600 | tf_op jit(solution)/shard_map/kab,kjbc->kjac/dot_general | solution.py:16
  73.4 5.5 %copy.31 = f32[8,8,128,128]{3,0,2,1:T(8,128)} copy(f32[8,8,128,128]{2,3,1,0:T(8,128)} %convolution_bitcast_fusion) | data formatting | bytes 8388608 | tf_op jit(solution)/shard_map/kab,kjbc->kjac/transpose | solution.py:16
  78.9 2.8 %convolution_bitcast_fusion.1 = f32[8,8,128,128]{2,3,1,0:T(8,128)} fusion(bf16[8,8,128,128]{3,2,1,0:T(8,128)(2,1)S(1)} %copy-done, bf16[4,8,128,128]{3,2,1,0:T(8,128)(2,1)S(1)} %copy-done.4), kind=kOutput, calls=%fused_computation.1 | convolution fusion | flops 268435456 | bytes 6553600 | tf_op jit(solution)/shard_map/kab,kjbc->kjac/dot_general | solution.py:16
  81.7 5.4 %copy.26 = f32[8,8,128,128]{3,0,2,1:T(8,128)} copy(f32[8,8,128,128]{2,3,1,0:T(8,128)} %convolution_bitcast_fusion.1) | data formatting | bytes 8388608 | tf_op jit(solution)/shard_map/kab,kjbc->kjac/transpose | solution.py:16
  87.1 2.7 %convolution_bitcast_fusion.2 = f32[8,8,128,128]{2,3,1,0:T(8,128)} fusion(bf16[8,8,128,128]{3,2,1,0:T(8,128)(2,1)S(1)} %copy-done, bf16[4,8,128,128]{3,2,1,0:T(8,128)(2,1)S(1)} %copy-done.4), kind=kOutput, calls=%fused_computation.2 | convolution fusion | flops 268435456 | bytes 6553600 | tf_op jit(solution)/shard_map/kab,kjbc->kjac/dot_general | solution.py:16
  89.8 5.4 %copy.21 = f32[8,8,128,128]{3,0,2,1:T(8,128)} copy(f32[8,8,128,128]{2,3,1,0:T(8,128)} %convolution_bitcast_fusion.2) | data formatting | bytes 8388608 | tf_op jit(solution)/shard_map/kab,kjbc->kjac/transpose | solution.py:16
  95.2 2.7 %convolution_bitcast_fusion.3 = f32[8,8,128,128]{2,3,1,0:T(8,128)} fusion(bf16[8,8,128,128]{3,2,1,0:T(8,128)(2,1)S(1)} %copy-done, bf16[4,8,128,128]{3,2,1,0:T(8,128)(2,1)S(1)} %copy-done.4), kind=kOutput, calls=%fused_computation.3 | convolution fusion | flops 268435456 | bytes 6553600 | tf_op jit(solution)/shard_map/kab,kjbc->kjac/dot_general | solution.py:16
  98.0 5.3 %copy.16 = f32[8,8,128,128]{3,0,2,1:T(8,128)} copy(f32[8,8,128,128]{2,3,1,0:T(8,128)} %convolution_bitcast_fusion.3) | data formatting | bytes 8388608 | tf_op jit(solution)/shard_map/kab,kjbc->kjac/transpose | solution.py:16
  103.3 6.1 %fusion.4 = f32[8,1,128,128]{3,1,2,0:T(1,128)S(1)} fusion(f32[8,8,1,1]{1,2,3,0:T(1,128)S(1)} %bitcast.85, f32[8,8,128,128]{3,0,2,1:T(8,128)} %copy.31), kind=kOutput, calls=%fused_computation.18 | convolution fusion | flops 12582912 | bytes 4718848 | tf_op jit(solution)/shard_map/jk,kjac->jac/dot_general | solution.py:23
  109.5 3.7 %fusion.3 = f32[8,1,128,128]{3,1,2,0:T(1,128)S(1)} fusion(f32[8,8,1,1]{1,2,3,0:T(1,128)S(1)} %bitcast.84, f32[8,8,128,128]{3,0,2,1:T(8,128)S(1)} %copy-done.1), kind=kOutput, calls=%fused_computation.17 | convolution fusion | flops 12582912 | bytes 4718848 | tf_op jit(solution)/shard_map/jk,kjac->jac/dot_general | solution.py:23
  113.2 3.7 %fusion.2 = f32[8,1,128,128]{3,1,2,0:T(1,128)S(1)} fusion(f32[8,8,1,1]{1,2,3,0:T(1,128)S(1)} %bitcast.83, f32[8,8,128,128]{3,0,2,1:T(8,128)S(1)} %copy-done.2), kind=kOutput, calls=%fused_computation.16 | convolution fusion | flops 12582912 | bytes 4718848 | tf_op jit(solution)/shard_map/jk,kjac->jac/dot_general | solution.py:23
  117.0 3.7 %fusion.1 = f32[8,1,128,128]{3,1,2,0:T(1,128)S(1)} fusion(f32[8,8,1,1]{1,2,3,0:T(1,128)S(1)} %bitcast.82, f32[8,8,128,128]{3,0,2,1:T(8,128)S(1)} %copy-done.3), kind=kOutput, calls=%fused_computation.15 | convolution fusion | flops 12582912 | bytes 4718848 | tf_op jit(solution)/shard_map/jk,kjac->jac/dot_general | solution.py:23
  120.7 1.5 %pad_maximum_fusion = f32[4,8,128,128]{3,2,1,0:T(8,128)} fusion(f32[1,8,128,128]{3,2,1,0:T(8,128)S(1)} %bitcast.78, f32[1,8,128,128]{3,2,1,0:T(8,128)S(1)} %bitcast.79, f32[1,8,128,128]{3,2,1,0:T(8,128)S(1)} %bitcast.80, f32[1,8,128,128]{3,2,1,0:T(8,128)S(1)} %bitcast.81), kind=kLoop, calls=%fused_computation.4 | loop fusion | flops 1572864 | bytes 4194304 | tf_op jit(solution)/shard_map/stack | solution.py:27
  (12 shorter events, 0.0 us)
Async XLA Ops:
  6.5 33.4 %all-gather.5.cloned.1.call-start = ((), (), s32[]{:S(2)}) async-start(), calls=%async_computation.1 | async-start | bytes 1310720 | tf_op jit(solution)/shard_map/all_gather | solution.py:32
  9.1 59.9 %all-gather.3.cloned.1.call-start = ((), (), s32[]{:S(2)}) async-start(), calls=%async_computation | async-start | bytes 2359296 | tf_op jit(solution)/shard_map/all_gather | solution.py:34
  73.4 5.5 %copy-start = (bf16[8,8,128,128]{3,2,1,0:T(8,128)(2,1)S(1)}, bf16[8,8,128,128]{3,2,1,0:T(8,128)(2,1)}, u32[]{:S(2)}) copy-start(bf16[8,8,128,128]{3,2,1,0:T(8,128)(2,1)} %all-gather.3.cloned.1.call-done) | copy-start | bytes 6291460
  73.4 5.5 %copy-start.4 = (bf16[4,8,128,128]{3,2,1,0:T(8,128)(2,1)S(1)}, bf16[4,8,128,128]{3,2,1,0:T(8,128)(2,1)}, u32[]{:S(2)}) copy-start(bf16[4,8,128,128]{3,2,1,0:T(8,128)(2,1)} %all-gather.5.cloned.1.call-done) | copy-start | bytes 3145732
  103.3 6.1 %copy-start.1 = (f32[8,8,128,128]{3,0,2,1:T(8,128)S(1)}, f32[8,8,128,128]{3,0,2,1:T(8,128)}, u32[]{:S(2)}) copy-start(f32[8,8,128,128]{3,0,2,1:T(8,128)} %copy.26) | copy-start | bytes 12582916
  103.3 9.9 %copy-start.2 = (f32[8,8,128,128]{3,0,2,1:T(8,128)S(1)}, f32[8,8,128,128]{3,0,2,1:T(8,128)}, u32[]{:S(2)}) copy-start(f32[8,8,128,128]{3,0,2,1:T(8,128)} %copy.21) | copy-start | bytes 12582916
  109.4 7.5 %copy-start.3 = (f32[8,8,128,128]{3,0,2,1:T(8,128)S(1)}, f32[8,8,128,128]{3,0,2,1:T(8,128)}, u32[]{:S(2)}) copy-start(f32[8,8,128,128]{3,0,2,1:T(8,128)} %copy.16) | copy-start | bytes 12582916
Sparse Core Ops, SparseCore 0:
  9.2 30.6 all-gather.4
  41.8 27.1 all-gather.2
where the time goes:
time: 129 us
  waiting for transfers between devices  56.6 us (44%)
  matrix products  30 us (23%)
  local copies, waits for them, and re-layouts  21.8 us (17%)
  between operations  13.5 us (10%)
  other arithmetic  7.1 us (6%)
    all_gather x1, waiting for transfers between devices, on_device(): later_full = lax.all_gather(masked_late, 'row', axis=0, tiled=True)  29.1 us
    all_gather x1, waiting for transfers between devices, on_device(): earlier_full = lax.all_gather(masked_early, 'col', axis=1, tiled=True)  27.5 us
    transpose x4, local copies, waits for them, and re-layouts, compose_blocks(): jnp.einsum('kab,kjbc->kjac', earlier_full[row_number], later_full, prefer...  21.6 us
    dot_general x4, matrix products, compose_blocks(): jnp.einsum('jk,kjac->jac', counts[row_number], products, precision=lax.Pr...  17.3 us
    dot_general x4, matrix products, compose_blocks(): jnp.einsum('kab,kjbc->kjac', earlier_full[row_number], later_full, prefer...  12.6 us
  transfers between devices with their start and end apart: 2, of which 2 were waited for; matrix products, arithmetic and copies ran while one was open for 3% of the time, Pallas kernels for 0%

commit v1 on v0

--- a/solution.py
+++ b/solution.py
@@ -31,7 +31,9 @@
     masked_early = earlier_blocks * earlier_pattern[:, :, None, None].astype(earlier_blocks.dtype)
     earlier_full = lax.all_gather(masked_early, "col", axis=1, tiled=True)
     masked_late = later_blocks * later_pattern[:, :, None, None].astype(later_blocks.dtype)
-    later_full = lax.all_gather(masked_late, "row", axis=0, tiled=True)
+    later_full = jnp.concatenate(
+        lax.all_to_all(jnp.stack([masked_late] * lax.axis_size("row")), "row", 0, 0), axis=0
+    )
     return compose_blocks(earlier_full, later_full, triples)
 
 

time: 129 us -> 107 us (0.83)
  waiting for transfers between devices: 56.6 us -> 31 us
  starting transfers between devices: 0.04 us -> 5.24 us
  other arithmetic: 7.1 us -> 4.11 us
  local copies, waits for them, and re-layouts: 21.8 us -> 23.5 us
    all_gather x1 -> x0, waiting for transfers between devices: 29.1 us -> none  [on_device(): later_full = lax.all_gather(masked_late, 'row', axis=0, tiled=True)]
    all_to_all x0 -> x1, starting transfers between devices: none -> 5.2 us  [on_device(): lax.all_to_all(jnp.stack([masked_late] * lax.axis_size('row')), 'row', 0, 0)]
    all_gather x1, waiting for transfers between devices: 27.5 us -> 31 us  [on_device(): earlier_full = lax.all_gather(masked_early, 'col', axis=1, tiled=True)]
    another operation x0 -> x1, local copies, waits for them, and re-layouts: none -> 1.83 us  [on_device(): jnp.stack([masked_late] * lax.axis_size('row'))]
  transfers between devices with their start and end apart: 2 -> 2, of which waited for: 2 -> 1; matrix products, arithmetic and copies ran while one was open for 3% -> 1% of each run, Pallas kernels for 0% -> 0%
where the time goes in v1:
time: 107 us
  waiting for transfers between devices  31 us (29%)
  matrix products  29.3 us (27%)
  local copies, waits for them, and re-layouts  23.5 us (22%)
  between operations  13.5 us (13%)
  starting transfers between devices  5.24 us (5%)
  other arithmetic  4.11 us (4%)
    all_gather x1, waiting for transfers between devices, on_device(): earlier_full = lax.all_gather(masked_early, 'col', axis=1, tiled=True)  31 us
    transpose x4, local copies, waits for them, and re-layouts, compose_blocks(): jnp.einsum('kab,kjbc->kjac', earlier_full[row_number], later_full, prefer...  21.6 us
    dot_general x4, matrix products, compose_blocks(): jnp.einsum('jk,kjac->jac', counts[row_number], products, precision=lax.Pr...  17.3 us
    dot_general x4, matrix products, compose_blocks(): jnp.einsum('kab,kjbc->kjac', earlier_full[row_number], later_full, prefer...  12 us
    all_to_all x1, starting transfers between devices, on_device(): lax.all_to_all(jnp.stack([masked_late] * lax.axis_size('row')), 'row', 0, 0)  5.2 us
  transfers between devices with their start and end apart: 2, of which 1 were waited for; matrix products, arithmetic and copies ran while one was open for 1% of the time, Pallas kernels for 0%

profile of v1, /device:TPU:0, one launch (start us, length us, event | category | flops | bytes accessed | tf_op | source)
XLA Modules:
  0.0 106.7 jit_solution(12155650640816232257)
XLA Ops:
  6.5 0.7 convert_bitcast_fusion
  7.2 1.0 multiply_bitcast_fusion
  8.3 1.8 %stack.12 = bf16[8,1,8,128,128]{4,3,2,1,0:T(8,128)(2,1)} broadcast(bf16[8,128,128]{2,1,0:T(8,128)(2,1)S(1)} %multiply_bitcast_fusion), dimensions={2,3,4} | broadcast | bytes 2359296 | tf_op jit(solution)/shard_map/stack | solution.py:35
  10.1 5.2 %all-to-all-start = ((bf16[8,1,8,128,128]{4,3,2,1,0:T(8,128)(2,1)}), bf16[8,1,8,128,128]{4,3,2,1,0:T(8,128)(2,1)S(1)}, u32[]{:S(2)}, u32[]{:S(2)}) async-start(bf16[8,1,8,128,128]{4,3,2,1,0:T(8,128)(2,1)} %stack.12), calls=%async_computation | async-start | bytes 4194304 | tf_op jit(solution)/shard_map/all_to_all | solution.py:35
  15.3 0.0 all-gather.2.cloned.1.call-start
  15.4 0.1 copy.7
  15.5 0.8 broadcast_multiply_fusion
  16.3 0.0 all-gather.2.cloned.1.call-update
  16.3 0.1 convert_reduce_fusion
  16.4 31.0 %all-gather.2.cloned.1.call-done = bf16[4,8,128,128]{3,2,1,0:T(8,128)(2,1)} async-done(((bf16[4,2,128,128]{3,2,1,0:T(8,128)(2,1)}), bf16[4,8,128,128]{3,2,1,0:T(8,128)(2,1)}) %all-gather.2.cloned.1.call-update) | async-done | bytes 1048592 | tf_op jit(solution)/shard_map/all_gather | solution.py:32
  47.4 0.0 all-to-all-done
  47.4 3.7 %convolution_bitcast_fusion.2 = f32[8,8,128,128]{2,3,1,0:T(8,128)} fusion(bf16[8,1,8,128,128]{4,3,2,1,0:T(8,128)(2,1)S(1)} %all-to-all-done, bf16[4,8,128,128]{3,2,1,0:T(8,128)(2,1)} %all-gather.2.cloned.1.call-done), kind=kOutput, calls=%fused_computation.2 | convolution fusion | flops 268435456 | bytes 6553600 | tf_op jit(solution)/shard_map/kab,kjbc->kjac/dot_general | solution.py:16
  51.2 5.5 %copy.14 = f32[8,8,128,128]{3,0,2,1:T(8,128)} copy(f32[8,8,128,128]{2,3,1,0:T(8,128)} %convolution_bitcast_fusion.2) | data formatting | bytes 8388608 | tf_op jit(solution)/shard_map/kab,kjbc->kjac/transpose | solution.py:16
  56.6 2.8 %convolution_bitcast_fusion.1 = f32[8,8,128,128]{2,3,1,0:T(8,128)} fusion(bf16[8,1,8,128,128]{4,3,2,1,0:T(8,128)(2,1)S(1)} %all-to-all-done, bf16[4,8,128,128]{3,2,1,0:T(8,128)(2,1)S(1)} %copy-done.3), kind=kOutput, calls=%fused_computation.1 | convolution fusion | flops 268435456 | bytes 6553600 | tf_op jit(solution)/shard_map/kab,kjbc->kjac/dot_general | solution.py:16
  59.4 5.4 %copy.18 = f32[8,8,128,128]{3,0,2,1:T(8,128)} copy(f32[8,8,128,128]{2,3,1,0:T(8,128)} %convolution_bitcast_fusion.1) | data formatting | bytes 8388608 | tf_op jit(solution)/shard_map/kab,kjbc->kjac/transpose | solution.py:16
  64.8 2.7 %convolution_bitcast_fusion = f32[8,8,128,128]{2,3,1,0:T(8,128)} fusion(bf16[8,1,8,128,128]{4,3,2,1,0:T(8,128)(2,1)S(1)} %all-to-all-done, bf16[4,8,128,128]{3,2,1,0:T(8,128)(2,1)S(1)} %copy-done.3), kind=kOutput, calls=%fused_computation | convolution fusion | flops 268435456 | bytes 6553600 | tf_op jit(solution)/shard_map/kab,kjbc->kjac/dot_general | solution.py:16
  67.5 5.4 %copy.22 = f32[8,8,128,128]{3,0,2,1:T(8,128)} copy(f32[8,8,128,128]{2,3,1,0:T(8,128)} %convolution_bitcast_fusion) | data formatting | bytes 8388608 | tf_op jit(solution)/shard_map/kab,kjbc->kjac/transpose | solution.py:16
  72.9 2.8 %convolution_bitcast_fusion.3 = f32[8,8,128,128]{2,3,1,0:T(8,128)} fusion(bf16[8,1,8,128,128]{4,3,2,1,0:T(8,128)(2,1)S(1)} %all-to-all-done, bf16[4,8,128,128]{3,2,1,0:T(8,128)(2,1)S(1)} %copy-done.3), kind=kOutput, calls=%fused_computation.3 | convolution fusion | flops 268435456 | bytes 6553600 | tf_op jit(solution)/shard_map/kab,kjbc->kjac/dot_general | solution.py:16
  75.6 5.3 %copy.10 = f32[8,8,128,128]{3,0,2,1:T(8,128)} copy(f32[8,8,128,128]{2,3,1,0:T(8,128)} %convolution_bitcast_fusion.3) | data formatting | bytes 8388608 | tf_op jit(solution)/shard_map/kab,kjbc->kjac/transpose | solution.py:16
  81.0 6.1 %fusion.6 = f32[8,1,128,128]{3,1,2,0:T(1,128)S(1)} fusion(f32[8,8,1,1]{1,2,3,0:T(1,128)S(1)} %bitcast.92, f32[8,8,128,128]{3,0,2,1:T(8,128)} %copy.14), kind=kOutput, calls=%fused_computation.20 | convolution fusion | flops 12582912 | bytes 4718848 | tf_op jit(solution)/shard_map/jk,kjac->jac/dot_general | solution.py:23
  87.1 3.7 %fusion.7 = f32[8,1,128,128]{3,1,2,0:T(1,128)S(1)} fusion(f32[8,8,1,1]{1,2,3,0:T(1,128)S(1)} %bitcast.91, f32[8,8,128,128]{3,0,2,1:T(8,128)S(1)} %copy-done), kind=kOutput, calls=%fused_computation.21 | convolution fusion | flops 12582912 | bytes 4718848 | tf_op jit(solution)/shard_map/jk,kjac->jac/dot_general | solution.py:23
  90.9 3.7 %fusion.8 = f32[8,1,128,128]{3,1,2,0:T(1,128)S(1)} fusion(f32[8,8,1,1]{1,2,3,0:T(1,128)S(1)} %bitcast.90, f32[8,8,128,128]{3,0,2,1:T(8,128)S(1)} %copy-done.1), kind=kOutput, calls=%fused_computation.22 | convolution fusion | flops 12582912 | bytes 4718848 | tf_op jit(solution)/shard_map/jk,kjac->jac/dot_general | solution.py:23
  94.6 3.7 %fusion.5 = f32[8,1,128,128]{3,1,2,0:T(1,128)S(1)} fusion(f32[8,8,1,1]{1,2,3,0:T(1,128)S(1)} %bitcast.89, f32[8,8,128,128]{3,0,2,1:T(8,128)S(1)} %copy-done.2), kind=kOutput, calls=%fused_computation.19 | convolution fusion | flops 12582912 | bytes 4718848 | tf_op jit(solution)/shard_map/jk,kjac->jac/dot_general | solution.py:23
  98.4 1.5 %pad_maximum_fusion = f32[4,8,128,128]{3,2,1,0:T(8,128)} fusion(f32[1,8,128,128]{3,2,1,0:T(8,128)S(1)} %bitcast.87, f32[1,8,128,128]{3,2,1,0:T(8,128)S(1)} %bitcast.86, f32[1,8,128,128]{3,2,1,0:T(8,128)S(1)} %bitcast.85, f32[1,8,128,128]{3,2,1,0:T(8,128)S(1)} %bitcast.88), kind=kLoop, calls=%fused_computation.4 | loop fusion | flops 1572864 | bytes 4194304 | tf_op jit(solution)/shard_map/stack | solution.py:27
  (16 shorter events, 0.0 us)
Async XLA Ops:
  6.5 8.8 %copy-start.6 = (s32[4,2]{0,1:T(2,128)S(1)}, s32[4,2]{0,1:T(2,128)}, u32[]{:S(2)}) copy-start(s32[4,2]{0,1:T(2,128)} %param.7) | copy-start | bytes 100
  6.5 8.9 %copy-start.4 = (bf16[4,2,128,128]{3,2,1,0:T(8,128)(2,1)S(1)}, bf16[4,2,128,128]{3,2,1,0:T(8,128)(2,1)}, u32[]{:S(2)}) copy-start(bf16[4,2,128,128]{3,2,1,0:T(8,128)(2,1)} %param.5) | copy-start | bytes 786436
  6.5 9.8 %copy-start.5 = (s32[4,8,48]{2,1,0:T(8,128)S(1)}, s32[4,8,48]{2,1,0:T(8,128)}, u32[]{:S(2)}) copy-start(s32[4,8,48]{2,1,0:T(8,128)} %param.9) | copy-start | bytes 18436
  10.1 37.3 %all-to-all-start = ((bf16[8,1,8,128,128]{4,3,2,1,0:T(8,128)(2,1)}), bf16[8,1,8,128,128]{4,3,2,1,0:T(8,128)(2,1)S(1)}, u32[]{:S(2)}, u32[]{:S(2)}) async-start(bf16[8,1,8,128,128]{4,3,2,1,0:T(8,128)(2,1)} %stack.12), calls=%async_computation | async-start | bytes 4194304 | tf_op jit(solution)/shard_map/all_to_all | solution.py:35
  15.3 32.1 %all-gather.2.cloned.1.call-start = ((), (), s32[]{:S(2)}) async-start(), calls=%async_computation.1 | async-start | bytes 1310720 | tf_op jit(solution)/shard_map/all_gather | solution.py:32
  51.1 5.5 %copy-start.3 = (bf16[4,8,128,128]{3,2,1,0:T(8,128)(2,1)S(1)}, bf16[4,8,128,128]{3,2,1,0:T(8,128)(2,1)}, u32[]{:S(2)}) copy-start(bf16[4,8,128,128]{3,2,1,0:T(8,128)(2,1)} %all-gather.2.cloned.1.call-done) | copy-start | bytes 3145732
  81.0 6.1 %copy-start = (f32[8,8,128,128]{3,0,2,1:T(8,128)S(1)}, f32[8,8,128,128]{3,0,2,1:T(8,128)}, u32[]{:S(2)}) copy-start(f32[8,8,128,128]{3,0,2,1:T(8,128)} %copy.18) | copy-start | bytes 12582916
  81.0 9.9 %copy-start.1 = (f32[8,8,128,128]{3,0,2,1:T(8,128)S(1)}, f32[8,8,128,128]{3,0,2,1:T(8,128)}, u32[]{:S(2)}) copy-start(f32[8,8,128,128]{3,0,2,1:T(8,128)} %copy.22) | copy-start | bytes 12582916
  87.1 7.5 %copy-start.2 = (f32[8,8,128,128]{3,0,2,1:T(8,128)S(1)}, f32[8,8,128,128]{3,0,2,1:T(8,128)}, u32[]{:S(2)}) copy-start(f32[8,8,128,128]{3,0,2,1:T(8,128)} %copy.10) | copy-start | bytes 12582916
Sparse Core Ops, SparseCore 0:
  17.7 29.6 all-gather.1
